TPU v7x, 32 devices: a whole 2x2x4 slice. The times are simulated.
32 devices in a mesh: dp: 8 (over y, x, core), tp: 4 (over z).
Axes of the slice: x: 2, y: 2, z: 4, core: 2. Of those that a mesh axis runs over, the one named last changes fastest.
Arguments:
- block_in: bfloat16 [128, 4, 37632], P('dp', 'tp'), may hold values from -6 to 6
- ln1_gain: float32 [768], P('tp'), may hold values from 0.1 to 1.9
- ln1_shift: float32 [768], P('tp'), may hold values from -1.75 to 1.75
- tok_w1: float32 [196, 384], replicated, may hold values from -0.4375 to 0.4375
- tok_b1: float32 [384], replicated, may hold values from -1.75 to 1.75
- tok_w2: float32 [384, 196], replicated, may hold values from -0.3125 to 0.3125
- tok_b2: float32 [196], replicated, may hold values from -1.75 to 1.75
- ln2_gain: float32 [768], P('tp'), may hold values from 0.1 to 1.9
- ln2_shift: float32 [768], P('tp'), may hold values from -1.75 to 1.75
- ch_w1: float32 [768, 3072], P('dp', 'tp'), may hold values from -0.21875 to 0.21875
- ch_b1: float32 [3072], replicated, may hold values from -1.75 to 1.75
- ch_w2: float32 [3072, 768], P('tp', 'dp'), may hold values from -0.109375 to 0.109375
- ch_b2: float32 [768], replicated, may hold values from -1.75 to 1.75
- group_ids: int32 [128], P('dp'), may hold values from 0 to 63
- out_grad: bfloat16 [128, 4, 37632], P('dp', 'tp'), may hold values from -6 to 6
Outputs:
- block_out: bfloat16 [128, 4, 37632], P('dp', 'tp')
- dx: bfloat16 [128, 4, 37632], P('dp', 'tp')
- group_norms: float32 [64], replicated
- d_ln1_gain: float32 [768], P('tp')
- d_ln1_shift: float32 [768], P('tp')
- d_tok_w1: float32 [196, 384], replicated
- d_tok_b1: float32 [384], replicated
- d_tok_w2: float32 [384, 196], replicated
- d_tok_b2: float32 [196], replicated
- d_ln2_gain: float32 [768], P('tp')
- d_ln2_shift: float32 [768], P('tp')
- d_ch_w1: float32 [768, 3072], P('dp', 'tp')
- d_ch_b1: float32 [3072], replicated
- d_ch_w2: float32 [3072, 768], P('tp', 'dp')
- d_ch_b2: float32 [768], replicated
All inputs are finite; a program needn't handle non-finite values.
Results may differ from a plain program's by a relative error of at most 0.01.
Values may be sent and summed in bfloat16 or wider, within the bound.
A program may use at most 128 MiB of HBM per device.

v0:
```python
import math
import jax
import jax.numpy as jnp
from jax import lax
from jax.sharding import PartitionSpec as P

S = 196
GROUPS = 64
epsilon = 1e-06
highest = lax.Precision.HIGHEST


def in_blocks(array, dim, size):
    lengths = array.shape
    tiles = array.reshape(*lengths[:dim], size, lengths[dim] // size, *lengths[dim + 1 :])
    return jnp.moveaxis(tiles, dim, 0)


def sum_at_owner(array, axis, dim):
    size = lax.axis_size(axis)
    tiles = lax.all_to_all(in_blocks(array, dim, size), axis, 0, 0, tiled=True)
    return jnp.sum(tiles.astype(jnp.float32), axis=0)


def norm_stats(values, full_width):
    totals = lax.psum((jnp.sum(values, -1), jnp.sum(values * values, -1)), "tp")
    average = totals[0] / full_width
    inverse = lax.rsqrt(totals[1] / full_width - average * average + epsilon)
    return ((values - average[..., None]) * inverse[..., None], inverse)


def norm_back(grad_hat, normed, inverse, full_width):
    totals = lax.psum((jnp.sum(grad_hat, -1), jnp.sum(grad_hat * normed, -1)), "tp")
    return inverse[..., None] * (
        grad_hat - totals[0][..., None] / full_width - normed * totals[1][..., None] / full_width
    )


def spread_slot(values, slot_mask):
    expanded = values[..., None, :] * slot_mask[:, None]
    return expanded.reshape(values.shape[:-1] + (slot_mask.shape[0] * values.shape[-1],))


def gather_channels(values):
    return lax.all_gather(values, "tp", axis=1, tiled=True)


def sum_channels(values):
    return lax.psum_scatter(
        values.astype(jnp.bfloat16), "tp", scatter_dimension=1, tiled=True
    ).astype(jnp.float32)


def per_device(
    block_in,
    ln1_gain,
    ln1_shift,
    tok_w1,
    tok_b1,
    tok_w2,
    tok_b2,
    ln2_gain,
    ln2_shift,
    ch_w1,
    ch_b1,
    ch_w2,
    ch_b2,
    group_ids,
    out_grad,
):
    f32 = jnp.float32
    bf16 = jnp.bfloat16
    images = block_in.shape[0]
    patches = S
    plain_in = block_in.reshape(images, patches, -1)
    plain_grad = out_grad.reshape(images, patches, -1)
    local_width = plain_in.shape[2]
    tp_count = lax.axis_size("tp")
    dp_count = lax.axis_size("dp")
    tp_place = lax.axis_index("tp")
    full_width = local_width * tp_count
    slot_mask = (jnp.arange(tp_count) == tp_place).astype(f32)
    row_count = images * patches
    input_float = plain_in.astype(f32)
    normed_one, inverse_one = norm_stats(input_float, full_width)
    mixed_in = (normed_one * ln1_gain + ln1_shift).astype(bf16)
    token_w1 = tok_w1.astype(bf16)
    token_w2 = tok_w2.astype(bf16)
    pre_act = jnp.einsum("nsc,sk->nck", mixed_in, token_w1, preferred_element_type=f32) + tok_b1
    hidden_act, gelu_token = jax.vjp(jax.nn.gelu, pre_act)
    hidden_low = hidden_act.astype(bf16)
    token_out = (
        jnp.einsum("nck,ks->nsc", hidden_low, token_w2, preferred_element_type=f32)
        + tok_b2[None, :, None]
    )
    residual = input_float + token_out
    normed_two, inverse_two = norm_stats(residual, full_width)
    branch_in = (normed_two * ln2_gain + ln2_shift).astype(bf16).reshape(row_count, local_width)
    grad_low = plain_grad.reshape(row_count, local_width)
    upper_rows, lower_rows = (
        lax.all_gather(ch_w1.astype(bf16), "dp", axis=0, tiled=True),
        lax.all_gather(ch_w2.astype(bf16), "dp", axis=1, tiled=True),
    )
    gathered = gather_channels(branch_in)
    hidden_width = upper_rows.shape[1]
    bias_first = lax.dynamic_slice_in_dim(ch_b1, tp_place * hidden_width, hidden_width)
    bias_second = lax.dynamic_slice_in_dim(ch_b2, tp_place * local_width, local_width)
    inner_act = jnp.dot(gathered, upper_rows, preferred_element_type=f32) + bias_first
    activated, gelu_branch = jax.vjp(jax.nn.gelu, inner_act)
    activated_low = activated.astype(bf16)
    branch_sum = (
        sum_channels(jnp.dot(activated_low, lower_rows, preferred_element_type=f32)) + bias_second
    )
    branch_low = branch_sum.astype(bf16)
    grad_full = gather_channels(grad_low)
    grad_activated = jnp.dot(grad_full, lower_rows.T, preferred_element_type=f32)
    grad_lower = jnp.dot(activated_low.T, grad_full, preferred_element_type=f32)
    grad_inner = gelu_branch(grad_activated)[0].astype(bf16)
    grad_upper = jnp.dot(gathered.T, grad_inner, preferred_element_type=f32)
    bias_first_grad = spread_slot(jnp.sum(grad_inner.astype(f32), 0), slot_mask)
    bias_second_grad = spread_slot(jnp.sum(grad_low.astype(f32), 0), slot_mask)
    grad_branch = sum_channels(jnp.dot(grad_inner, upper_rows.T, preferred_element_type=f32))
    upper_grad, lower_grad = (
        sum_at_owner(grad_upper.astype(jnp.bfloat16), "dp", 0),
        sum_at_owner(grad_lower.astype(jnp.bfloat16), "dp", 1),
    )
    output = (residual + branch_low.astype(f32).reshape(residual.shape)).astype(bf16)
    grad_normed = grad_branch.reshape(residual.shape)
    image_gain = jnp.sum(grad_normed * normed_two, 1)
    image_shift = jnp.sum(grad_normed, 1)
    grad_resid = plain_grad.astype(f32) + norm_back(
        grad_normed * ln2_gain, normed_two, inverse_two, full_width
    )
    grad_token_low = grad_resid.astype(bf16)
    grad_hidden = jnp.einsum("nsc,ks->nck", grad_token_low, token_w2, preferred_element_type=f32)
    token_w2_grad = jnp.einsum(
        "nck,nsc->ks", hidden_low, grad_token_low, preferred_element_type=f32
    )
    token_b2_grad = jnp.sum(grad_token_low.astype(f32), (0, 2))
    grad_pre = gelu_token(grad_hidden)[0].astype(bf16)
    token_w1_grad = jnp.einsum("nsc,nck->sk", mixed_in, grad_pre, preferred_element_type=f32)
    token_b1_grad = jnp.sum(grad_pre.astype(f32), (0, 1))
    grad_mixed = jnp.einsum("nck,sk->nsc", grad_pre, token_w1, preferred_element_type=f32)
    gain_one_grad = jnp.sum(grad_mixed * normed_one, (0, 1))
    shift_one_grad = jnp.sum(grad_mixed, (0, 1))
    grad_input = (
        grad_resid + norm_back(grad_mixed * ln1_gain, normed_one, inverse_one, full_width)
    ).astype(bf16)
    member = (group_ids[:, None] == jnp.arange(GROUPS)[None, :]).astype(f32)
    image_stats = jnp.stack([image_gain, image_shift], 1).reshape(images, 2 * local_width)
    group_local = jnp.dot(member.T, image_stats, precision=highest).reshape(GROUPS, 2, local_width)
    norm_one_local = jnp.stack([gain_one_grad, shift_one_grad], 0)
    totals = lax.psum(
        (
            token_w1_grad,
            token_b1_grad,
            token_w2_grad,
            token_b2_grad,
            spread_slot(group_local, slot_mask),
            spread_slot(norm_one_local, slot_mask),
            bias_first_grad,
            bias_second_grad,
        ),
        ("dp", "tp"),
    )
    group_full = totals[4]
    group_norms = jnp.sqrt(jnp.sum(group_full * group_full, (1, 2)))
    clip_bound = 2.0 * math.sqrt(images * dp_count * patches * full_width / GROUPS)
    factor = clip_bound / jnp.maximum(group_norms, clip_bound)
    clipped = jnp.sum(factor[:, None, None] * group_full, 0)
    clipped_local = lax.dynamic_slice_in_dim(clipped, tp_place * local_width, local_width, 1)
    norm_one_own = lax.dynamic_slice_in_dim(totals[5], tp_place * local_width, local_width, 1)
    stored_out = output.reshape(images, 1, patches * local_width)
    stored_grad = grad_input.reshape(images, 1, patches * local_width)
    return (
        stored_out,
        stored_grad,
        group_norms,
        norm_one_own[0],
        norm_one_own[1],
        totals[0],
        totals[1],
        totals[2],
        totals[3],
        clipped_local[0],
        clipped_local[1],
        upper_grad,
        totals[6],
        lower_grad,
        totals[7],
    )


def solution(mesh):
    in_specs = (
        P("dp", "tp", None),
        P("tp"),
        P("tp"),
        P(),
        P(),
        P(),
        P(),
        P("tp"),
        P("tp"),
        P("dp", "tp"),
        P(),
        P("tp", "dp"),
        P(),
        P("dp"),
        P("dp", "tp", None),
    )
    out_specs = (
        P("dp", "tp", None),
        P("dp", "tp", None),
        P(),
        P("tp"),
        P("tp"),
        P(),
        P(),
        P(),
        P(),
        P("tp"),
        P("tp"),
        P("dp", "tp"),
        P(),
        P("tp", "dp"),
        P(),
    )
    return jax.shard_map(
        per_device, mesh=mesh, in_specs=in_specs, out_specs=out_specs, check_vma=False
    )
```

profile of v0, /device:TPU:0, one launch (start us, length us, event | category | flops | bytes accessed | tf_op | source)
XLA Modules:
  0.0 688.9 jit_solution(15931302584527314932)
XLA Ops:
  15.6 20.9 %all-reduce.5 = (f32[16,196]{1,0:T(8,128)S(1)}, f32[16,196]{1,0:T(8,128)S(1)}) all-reduce(f32[16,196]{1,0:T(8,128)S(1)} %get-tuple-element.20, f32[16,196]{1,0:T(8,128)S(1)} %get-tuple-element.19), channel_id=1, replica_groups=mesh['dp'=8,'tp'=4] {'tp'}, use_global_device_ids=true, to_apply=%region_3.0 | all-reduce | flops 6272 | bytes 50176 | tf_op jit(solution)/shard_map/psum | solution.py:26
  44.6 15.8 %all-reduce.4 = (f32[16,196]{1,0:T(8,128)S(1)}, f32[16,196]{1,0:T(8,128)S(1)}) all-reduce(f32[16,196]{1,0:T(8,128)S(1)} %get-tuple-element.23, f32[16,196]{1,0:T(8,128)S(1)} %get-tuple-element.22), channel_id=1, replica_groups=mesh['dp'=8,'tp'=4] {'tp'}, use_global_device_ids=true, to_apply=%region_7.0 | all-reduce | flops 6272 | bytes 50176 | tf_op jit(solution)/shard_map/psum | solution.py:26
  76.0 84.4 %all-gather.5.cloned.1.call-done = bf16[3136,768]{0,1:T(8,128)(2,1)} async-done(((bf16[3136,192]{0,1:T(8,128)(2,1)}), bf16[3136,768]{0,1:T(8,128)(2,1)}) %all-gather.5.cloned.1.call-update) | async-done | bytes 4816912 | tf_op jit(solution)/shard_map/all_gather | solution.py:45
  160.4 10.4 %fusion.40 = f32[3136,768]{1,0:T(8,128)} fusion(bf16[3136,768]{0,1:T(8,128)(2,1)} %all-gather.5.cloned.1.call-done, bf16[768,768]{1,0:T(8,128)(2,1)} %all-gather.7.cloned.1.call-done), kind=kOutput, calls=%fused_computation.92 | convolution fusion | flops 3699376128 | bytes 15630336 | tf_op jit(solution)/shard_map/dot_general | solution.py:108
  170.8 14.6 %all-gather.9.cloned.1.call-done = bf16[768,768]{0,1:T(8,128)(2,1)} async-done(((bf16[768,96]{0,1:T(8,128)(2,1)}), bf16[768,768]{0,1:T(8,128)(2,1)}) %all-gather.9.cloned.1.call-update) | async-done | bytes 1179664 | tf_op jit(solution)/shard_map/all_gather | solution.py:102
  185.4 10.6 %convolution_convert_fusion.1 = bf16[3136,768]{0,1:T(8,128)(2,1)} fusion(bf16[768,768]{0,1:T(8,128)(2,1)} %all-gather.9.cloned.1.call-done, f32[3136,768]{1,0:T(8,128)} %fusion.40, f32[768]{0:T(1024)S(1)} %dynamic_slice.12), kind=kOutput, calls=%fused_computation.14 | convolution fusion | flops 3725869056 | bytes 15633408 | tf_op jit(solution)/shard_map/dot_general | solution.py:112
  196.4 83.0 %all-gather.11.cloned.1.call-done = bf16[3136,768]{0,1:T(8,128)(2,1)} async-done(((bf16[3136,192]{0,1:T(8,128)(2,1)}), bf16[3136,768]{0,1:T(8,128)(2,1)}) %all-gather.11.cloned.1.call-update) | async-done | bytes 4816912 | tf_op jit(solution)/shard_map/all_gather | solution.py:45
  279.5 15.2 %convert_reduce_fusion = (f32[768]{0:T(1024)S(1)}, bf16[3136,768]{1,0:T(8,128)(2,1)S(1)}) fusion(f32[3136,768]{1,0:T(8,128)} %fusion.40, f32[768]{0:T(1024)S(1)} %dynamic_slice.12, bf16[3136,768]{0,1:T(8,128)(2,1)} %all-gather.11.cloned.1.call-done, bf16[768,768]{0,1:T(8,128)(2,1)} %all-gather.9.cloned.1.call-done), kind=kOutput, calls=%fused_computation.9 | convolution fusion | flops 3754769664 | bytes 20453376 | tf_op jit(solution)/shard_map/dot_general | solution.py:116
  296.8 5.9 convolution_convert_fusion
  302.7 10.6 %convolution_convert_fusion.2 = bf16[768,768]{0,1:T(8,128)(2,1)} fusion(bf16[3136,768]{0,1:T(8,128)(2,1)} %all-gather.11.cloned.1.call-done, f32[3136,768]{1,0:T(8,128)} %fusion.40, f32[768]{0:T(1024)S(1)} %dynamic_slice.12), kind=kOutput, calls=%fused_computation.49 | convolution fusion | flops 3724050432 | bytes 15633408 | tf_op jit(solution)/shard_map/dot_general | solution.py:117
  317.8 9.1 %convolution_convert_fusion.3 = bf16[768,768]{1,0:T(8,128)(2,1)} fusion(bf16[3136,768]{0,1:T(8,128)(2,1)} %all-gather.5.cloned.1.call-done, bf16[3136,768]{1,0:T(8,128)(2,1)} %copy-done.29), kind=kOutput, calls=%fused_computation.50 | convolution fusion | flops 3699965952 | bytes 10813440 | tf_op jit(solution)/shard_map/dot_general | solution.py:119
  326.9 7.7 %all-to-all-done.1 = bf16[8,768,96]{1,2,0:T(8,128)(2,1)} async-done(((bf16[8,768,96]{1,2,0:T(8,128)(2,1)}), bf16[8,768,96]{1,2,0:T(8,128)(2,1)}, u32[]{:S(2)}, u32[]{:S(2)}) %all-to-all-start.1) | async-done | bytes 1179680 | tf_op jit(solution)/shard_map/all_to_all | solution.py:21
  341.9 4.8 copy.76
  357.9 10.7 %reduce-scatter.3.cloned.1.call-done = bf16[3136,192]{0,1:T(8,128)(2,1)} async-done(((bf16[3136,768]{0,1:T(8,128)(2,1)}), bf16[3136,192]{0,1:T(8,128)(2,1)}) %reduce-scatter.3.cloned.1.call-update) | async-done | bytes 1204240 | tf_op jit(solution)/shard_map/reduce_scatter | solution.py:49
  370.1 5.7 reshape.138
  375.8 84.1 %reduce-scatter.5.cloned.1.call-done = bf16[3136,192]{0,1:T(8,128)(2,1)} async-done(((bf16[3136,768]{0,1:T(8,128)(2,1)}), bf16[3136,192]{0,1:T(8,128)(2,1)}) %reduce-scatter.5.cloned.1.call-update) | async-done | bytes 1204240 | tf_op jit(solution)/shard_map/reduce_scatter | solution.py:49
  462.2 5.7 reshape.130
  472.7 19.7 %all-reduce.3 = (f32[16,196]{1,0:T(8,128)}, f32[16,196]{1,0:T(8,128)}) all-reduce(f32[16,196]{1,0:T(8,128)S(1)} %get-tuple-element.18, f32[16,196]{1,0:T(8,128)} %reduce_sum.187), channel_id=1, replica_groups=mesh['dp'=8,'tp'=4] {'tp'}, use_global_device_ids=true, to_apply=%region_13.0 | all-reduce | flops 6272 | bytes 50176 | tf_op jit(solution)/shard_map/psum | solution.py:33
  493.1 8.6 %convert_reduce_fusion.3 = (f32[196]{0:T(256)}, f32[16,196,192]{1,2,0:T(8,128)S(1)}, bf16[16,196,192]{1,2,0:T(8,128)(2,1)}) fusion(f32[16,196,192]{1,2,0:T(8,128)} %copy.76, f32[16,196]{1,0:T(8,128)} %get-tuple-element.34, f32[16,196,192]{1,2,0:T(8,128)} %copy-done.3, f32[16,196]{1,0:T(8,128)S(1)} %get-tuple-element.47, ...), kind=kLoop, calls=%fused_computation.32 | loop fusion | flops 8429372 | bytes 13298192 | tf_op jit(solution)/shard_map/reduce_sum | solution.py:139
  501.7 6.2 convolution_bitcast_fusion
  528.8 16.1 %all-reduce.2 = (f32[16,196]{1,0:T(8,128)S(1)}, f32[16,196]{1,0:T(8,128)S(1)}) all-reduce(f32[16,196]{1,0:T(8,128)S(1)} %get-tuple-element.16, f32[16,196]{1,0:T(8,128)S(1)} %get-tuple-element.21), channel_id=1, replica_groups=mesh['dp'=8,'tp'=4] {'tp'}, use_global_device_ids=true, to_apply=%region_17.0 | all-reduce | flops 6272 | bytes 50176 | tf_op jit(solution)/shard_map/psum | solution.py:33
  544.9 5.3 add_convert_fusion
  555.6 39.9 %all-reduce = (f32[2,768]{1,0:T(2,128)S(1)}, f32[384]{0:T(512)}, f32[196]{0:T(256)}, f32[3072]{0:T(1024)}, f32[768]{0:T(1024)}) all-reduce(f32[2,768]{1,0:T(2,128)S(1)} %broadcast_multiply_fusion.6, f32[384]{0:T(512)S(1)} %copy-done.19, f32[196]{0:T(256)S(1)} %copy-done.18, ...), channel_id=1, replica_groups=mesh['dp'=8,'tp'=4] {'dp','tp'}, use_global_device_ids=true, to_apply=%region_24.0 | all-reduce | flops 5956 | bytes 47648 | tf_op jit(solution)/shard_map/psum | solution.py:153
  595.5 79.3 %all-reduce.8.cloned.1.call-done = (f32[64,2,768]{2,0,1:T(8,128)}, f32[196,384]{1,0:T(8,128)}, f32[384,196]{0,1:T(8,128)}) async-done(((f32[64,2,768]{2,0,1:T(8,128)}, f32[196,384]{1,0:T(8,128)}, f32[384,196]{0,1:T(8,128)}), (f32[64,2,768]{2,0,1:T(8,128)}, f32[196,384]{1,0:T(8,128)}, f32[384,196]{0,1:T(8,128)})) %all-reduce.8.cloned.1.call-update) | async-done | bytes 995344 | tf_op jit(solution)/shard_map/psum | solution.py:153
  (146 shorter events, 99.7 us)
Async XLA Ops:
  7.2 68.8 %all-gather.7.cloned.1.call-start = ((), (), s32[]{:S(2)}) async-start(), calls=%async_computation.5 | async-start | bytes 1327104 | tf_op jit(solution)/shard_map/all_gather | solution.py:101
  8.9 151.5 %all-gather.5.cloned.1.call-start = ((), (), s32[]{:S(2)}) async-start(), calls=%async_computation.4 | async-start | bytes 6144000 | tf_op jit(solution)/shard_map/all_gather | solution.py:45
  12.3 24.2 %copy-start.15 = (f32[192]{0:T(256)S(1)}, f32[192]{0:T(256)}, u32[]{:S(2)}) copy-start(f32[192]{0:T(256)} %param.16) | copy-start | bytes 2308
  12.3 24.2 %copy-start.20 = (f32[192]{0:T(256)S(1)}, f32[192]{0:T(256)}, u32[]{:S(2)}) copy-start(f32[192]{0:T(256)} %param.17) | copy-start | bytes 2308
  15.6 24.6 %copy-start.10 = (f32[196,384]{1,0:T(8,128)S(1)}, f32[196,384]{1,0:T(8,128)}, u32[]{:S(2)}) copy-start(f32[196,384]{1,0:T(8,128)} %param.18) | copy-start | bytes 903172
  42.1 18.4 %copy-start.13 = (f32[192]{0:T(256)S(1)}, f32[192]{0:T(256)}, u32[]{:S(2)}) copy-start(f32[192]{0:T(256)} %param.22) | copy-start | bytes 2308
  44.6 19.2 %copy-start.3 = (f32[16,196,192]{1,2,0:T(8,128)}, f32[16,196,192]{1,2,0:T(8,128)S(1)}, u32[]{:S(2)}) copy-start(f32[16,196,192]{1,2,0:T(8,128)S(1)} %get-tuple-element.55) | copy-start | bytes 7225348
  68.1 117.2 %all-gather.9.cloned.1.call-start = ((), (), s32[]{:S(2)}) async-start(), calls=%async_computation.6 | async-start | bytes 1327104 | tf_op jit(solution)/shard_map/all_gather | solution.py:102
  69.8 209.6 %all-gather.11.cloned.1.call-start = ((), (), s32[]{:S(2)}) async-start(), calls=%async_computation.8 | async-start | bytes 6144000 | tf_op jit(solution)/shard_map/all_gather | solution.py:45
  74.9 293.6 %reduce-scatter.3.cloned.1.call-start = ((), (), s32[]{:S(2)}) async-start(), calls=%async_computation.7 | async-start | bytes 6144000 | tf_op jit(solution)/shard_map/reduce_scatter | solution.py:49
  196.0 100.9 %copy-start.23 = (bf16[768,768]{1,0:T(8,128)(2,1)S(1)}, bf16[768,768]{1,0:T(8,128)(2,1)}, u32[]{:S(2)}) copy-start(bf16[768,768]{1,0:T(8,128)(2,1)} %all-gather.7.cloned.1.call-done) | copy-start | bytes 3538948
  196.0 263.8 %reduce-scatter.5.cloned.1.call-start = ((), (), s32[]{:S(2)}) async-start(), calls=%async_computation.9 | async-start | bytes 6144000 | tf_op jit(solution)/shard_map/reduce_scatter | solution.py:49
  313.3 21.3 %all-to-all-start.1 = ((bf16[8,768,96]{1,2,0:T(8,128)(2,1)}), bf16[8,768,96]{1,2,0:T(8,128)(2,1)}, u32[]{:S(2)}, u32[]{:S(2)}) async-start(bf16[8,768,96]{1,2,0:T(8,128)(2,1)} %bitcast.18), calls=%async_computation.3 | async-start | bytes 2359296 | tf_op jit(solution)/shard_map/all_to_all | solution.py:21
  326.8 12.1 %copy-start.8 = (bf16[16,1,37632]{2,0,1:T(8,128)(2,1)S(1)}, bf16[16,1,37632]{2,0,1:T(8,128)(2,1)}, u32[]{:S(2)}) copy-start(bf16[16,1,37632]{2,0,1:T(8,128)(2,1)} %param.29) | copy-start | bytes 3612676
  334.6 21.1 %all-to-all-start = ((bf16[8,96,768]{2,1,0:T(8,128)(2,1)}), bf16[8,96,768]{2,1,0:T(8,128)(2,1)}, u32[]{:S(2)}, u32[]{:S(2)}) async-start(bf16[8,96,768]{2,1,0:T(8,128)(2,1)} %bitcast.81), calls=%async_computation.2 | async-start | bytes 2359296 | tf_op jit(solution)/shard_map/all_to_all | solution.py:21
  338.9 335.9 %all-reduce.8.cloned.1.call-start = ((), (), s32[]{:S(2)}) async-start(), calls=%async_computation.10 | async-start | bytes 2015232 | tf_op jit(solution)/shard_map/psum | solution.py:153
  370.0 89.8 %copy-start.14 = (f32[192]{0:T(256)S(1)}, f32[192]{0:T(256)}, u32[]{:S(2)}) copy-start(f32[192]{0:T(256)} %param.22) | copy-start | bytes 2308
  493.1 8.6 %copy-start.27 = (f32[384]{0:T(512)S(1)}, f32[384]{0:T(512)}, u32[]{:S(2)}) copy-start(f32[384]{0:T(512)} %param.19) | copy-start | bytes 4612
  493.1 14.8 %slice-start = ((s8[4718592]{0:T(1024)(128)(4,1)}), s8[4194304]{0:T(1024)(128)(4,1)S(1)}, s32[]{:S(2)}) async-start(s8[4718592]{0:T(1024)(128)(4,1)} %bitcast.79), calls=%async_computation.11 | async-start | bytes 8388608
  501.7 6.2 copy-start.4
  501.7 6.2 slice-start.1
  501.7 6.2 copy-start.25
  523.0 22.0 %copy-start.2 = (f32[16,196,192]{1,2,0:T(8,128)S(1)}, f32[16,196,192]{1,2,0:T(8,128)}, u32[]{:S(2)}) copy-start(f32[16,196,192]{1,2,0:T(8,128)} %copy.70) | copy-start | bytes 7225348
  523.0 22.0 %copy-start.17 = (f32[192]{0:T(256)S(1)}, f32[192]{0:T(256)}, u32[]{:S(2)}) copy-start(f32[192]{0:T(256)} %param.16) | copy-start | bytes 2308
  (17 other events, 51.9 us)
Sparse Core Ops, SparseCore 0:
  10.5 26.7 all-gather.6
  68.2 92.0 all-gather.4
  162.8 22.4 all-gather.8
  186.8 92.6 all-gather.10
  281.6 86.8 reduce-scatter.2
  370.8 88.9 reduce-scatter.4
  545.0 129.7 all-reduce.7
where the time goes:
time: 698 us; the launch traced here: 689 us
  waiting for transfers between devices  369 us (53%)
  blocking collectives  112 us (16%)
  matrix products  81.5 us (12%)
  local copies, waits for them, and re-layouts  59.5 us (9%)
  other arithmetic  42.3 us (6%)
  between operations  15 us (2%)
  starting transfers between devices  9.6 us (1%)
    all_gather x2, waiting for transfers between devices, gather_channels(): return lax.all_gather(values, 'tp', axis=1, tiled=True)  167 us
    reduce_scatter x2, waiting for transfers between devices, sum_channels(): lax.psum_scatter(values.astype(jnp.bfloat16), 'tp', scatter_dimension=1,...  94.7 us
    psum x1, waiting for transfers between devices, per_device(): lax.psum((token_w1_grad, token_b1_grad, token_w2_grad, token_b2_grad, spr...  79.3 us
    psum x1, blocking collectives, per_device(): lax.psum((token_w1_grad, token_b1_grad, token_w2_grad, token_b2_grad, spr...  39.9 us
    psum x2, blocking collectives, norm_stats(): totals = lax.psum((jnp.sum(values, -1), jnp.sum(values * values, -1)), 'tp')  36.8 us
    psum x2, blocking collectives, norm_back(): lax.psum((jnp.sum(grad_hat, -1), jnp.sum(grad_hat * normed, -1)), 'tp')  35.7 us
    dot_general x1, matrix products, per_device(): jnp.dot(grad_full, lower_rows.T, preferred_element_type=f32)  15.2 us
    all_gather x1, waiting for transfers between devices, per_device(): lax.all_gather(ch_w2.astype(bf16), 'dp', axis=1, tiled=True)  14.6 us
  transfers between devices with their start and end apart: 9, of which 8 were waited for; matrix products, arithmetic and copies ran while one was open for 18% of the time, Pallas kernels for 0%

commit v1 on v0

--- a/solution.py
+++ b/solution.py
@@ -8,6 +8,25 @@
 GROUPS = 64
 epsilon = 1e-06
 highest = lax.Precision.HIGHEST
+
+
+def collect(shard, axis, dim):
+    size, index, rows = (lax.axis_size(axis), lax.axis_index(axis), shard.shape[dim])
+    forward = [(i, (i + 1) % size) for i in range(size)]
+    backward = [(i, (i - 1) % size) for i in range(size)]
+    out = jnp.zeros((*shard.shape[:dim], size * rows, *shard.shape[dim + 1 :]), shard.dtype)
+    out = lax.dynamic_update_slice_in_dim(out, shard, index * rows, axis=dim)
+    from_left = from_right = shard
+    middle = size // 2
+    for hop in range(1, middle + 1):
+        from_left = lax.ppermute(from_left, axis, forward)
+        out = lax.dynamic_update_slice_in_dim(out, from_left, (index - hop) % size * rows, axis=dim)
+        if hop < size - middle:
+            from_right = lax.ppermute(from_right, axis, backward)
+            out = lax.dynamic_update_slice_in_dim(
+                out, from_right, (index + hop) % size * rows, axis=dim
+            )
+    return out
 
 
 def in_blocks(array, dim, size):
@@ -99,7 +118,7 @@
     grad_low = plain_grad.reshape(row_count, local_width)
     upper_rows, lower_rows = (
         lax.all_gather(ch_w1.astype(bf16), "dp", axis=0, tiled=True),
-        lax.all_gather(ch_w2.astype(bf16), "dp", axis=1, tiled=True),
+        collect(ch_w2.astype(bf16), "dp", 1),
     )
     gathered = gather_channels(branch_in)
     hidden_width = upper_rows.shape[1]

time: 698 us -> 672 us (0.963)
  waiting for transfers between devices: 369 us -> 339 us
  starting transfers between devices: 9.6 us -> 17.5 us
  matrix products: 81.5 us -> 73.8 us
    all_gather x2, waiting for transfers between devices: 167 us -> 137 us  [gather_channels(): return lax.all_gather(values, 'tp', axis=1, tiled=True)]
    ppermute x0 -> x7, waiting for transfers between devices: none -> 14.6 us  [the longest x4 14.6 us: collect(): from_left = lax.ppermute(from_left, axis, forward)]
    all_gather x1 -> x0, waiting for transfers between devices: 14.6 us -> none  [per_device(): lax.all_gather(ch_w2.astype(bf16), 'dp', axis=1, tiled=True)]
    ppermute x0 -> x7, starting transfers between devices: none -> 8.12 us  [the longest x3 7.91 us: collect(): from_right = lax.ppermute(from_right, axis, backward)]
  transfers between devices with their start and end apart: 9 -> 15, of which waited for: 8 -> 11; matrix products, arithmetic and copies ran while one was open for 18% -> 17% of each run, Pallas kernels for 0% -> 0%
where the time goes in v1:
time: 672 us; the launch traced here: 663 us
  waiting for transfers between devices  339 us (50%)
  blocking collectives  112 us (17%)
  matrix products  73.8 us (11%)
  local copies, waits for them, and re-layouts  63.8 us (9%)
  other arithmetic  41.4 us (6%)
  starting transfers between devices  17.5 us (3%)
  between operations  15.1 us (2%)
    all_gather x2, waiting for transfers between devices, gather_channels(): return lax.all_gather(values, 'tp', axis=1, tiled=True)  137 us
    reduce_scatter x2, waiting for transfers between devices, sum_channels(): lax.psum_scatter(values.astype(jnp.bfloat16), 'tp', scatter_dimension=1,...  94.8 us
    psum x1, waiting for transfers between devices, per_device(): lax.psum((token_w1_grad, token_b1_grad, token_w2_grad, token_b2_grad, spr...  79.3 us
    psum x1, blocking collectives, per_device(): lax.psum((token_w1_grad, token_b1_grad, token_w2_grad, token_b2_grad, spr...  39.9 us
    psum x2, blocking collectives, norm_stats(): totals = lax.psum((jnp.sum(values, -1), jnp.sum(values * values, -1)), 'tp')  36.8 us
    psum x2, blocking collectives, norm_back(): lax.psum((jnp.sum(grad_hat, -1), jnp.sum(grad_hat * normed, -1)), 'tp')  35.7 us
    dot_general x1, matrix products, per_device(): jnp.dot(grad_full, lower_rows.T, preferred_element_type=f32)  15.2 us
    ppermute x4, waiting for transfers between devices, collect(): from_left = lax.ppermute(from_left, axis, forward)  14.6 us
  transfers between devices with their start and end apart: 15, of which 11 were waited for; matrix products, arithmetic and copies ran while one was open for 17% of the time, Pallas kernels for 0%

profile of v1, /device:TPU:0, one launch (start us, length us, event | category | flops | bytes accessed | tf_op | source)
XLA Modules:
  0.0 662.5 jit_solution(5727268090882115338)
XLA Ops:
  15.6 20.9 %all-reduce.5 = (f32[16,196]{1,0:T(8,128)S(1)}, f32[16,196]{1,0:T(8,128)S(1)}) all-reduce(f32[16,196]{1,0:T(8,128)S(1)} %get-tuple-element.20, f32[16,196]{1,0:T(8,128)S(1)} %get-tuple-element.19), channel_id=1, replica_groups=mesh['dp'=8,'tp'=4] {'tp'}, use_global_device_ids=true, to_apply=%region_3.0 | all-reduce | flops 6272 | bytes 50176 | tf_op jit(solution)/shard_map/psum | solution.py:45
  44.6 15.8 %all-reduce.4 = (f32[16,196]{1,0:T(8,128)S(1)}, f32[16,196]{1,0:T(8,128)S(1)}) all-reduce(f32[16,196]{1,0:T(8,128)S(1)} %get-tuple-element.23, f32[16,196]{1,0:T(8,128)S(1)} %get-tuple-element.22), channel_id=1, replica_groups=mesh['dp'=8,'tp'=4] {'tp'}, use_global_device_ids=true, to_apply=%region_7.0 | all-reduce | flops 6272 | bytes 50176 | tf_op jit(solution)/shard_map/psum | solution.py:45
  92.3 5.4 collective-permute-done.6
  97.8 62.6 %all-gather.4.cloned.1.call-done = bf16[3136,768]{0,1:T(8,128)(2,1)} async-done(((bf16[3136,192]{0,1:T(8,128)(2,1)}), bf16[3136,768]{0,1:T(8,128)(2,1)}) %all-gather.4.cloned.1.call-update) | async-done | bytes 4816912 | tf_op jit(solution)/shard_map/all_gather | solution.py:64
  160.4 6.7 %fusion.42 = f32[3136,768]{1,0:T(8,128)S(1)} fusion(bf16[3136,768]{0,1:T(8,128)(2,1)} %all-gather.4.cloned.1.call-done, bf16[768,768]{1,0:T(8,128)(2,1)} %all-gather.6.cloned.1.call-done), kind=kOutput, calls=%fused_computation.105 | convolution fusion | flops 3699376128 | bytes 15630336 | tf_op jit(solution)/shard_map/dot_general | solution.py:127
  171.2 6.6 convolution_convert_fusion.1
  178.2 74.8 %all-gather.8.cloned.1.call-done = bf16[3136,768]{0,1:T(8,128)(2,1)} async-done(((bf16[3136,192]{0,1:T(8,128)(2,1)}), bf16[3136,768]{0,1:T(8,128)(2,1)}) %all-gather.8.cloned.1.call-update) | async-done | bytes 4816912 | tf_op jit(solution)/shard_map/all_gather | solution.py:64
  253.1 15.2 %convert_reduce_fusion = (f32[768]{0:T(1024)S(1)}, bf16[3136,768]{1,0:T(8,128)(2,1)S(1)}) fusion(f32[3136,768]{1,0:T(8,128)} %copy-done.30, f32[768]{0:T(1024)S(1)} %dynamic_slice.12, bf16[768,768]{0,1:T(8,128)(2,1)S(1)} %constant_dynamic-update-slice_fusion, bf16[3136,768]{0,1:T(8,128)(2,1)} %all-gather.8.cloned.1.call-done), kind=kOutput, calls=%fused_computation.14 | convolution fusion | flops 3754769664 | bytes 20453376 | tf_op jit(solution)/shard_map/dot_general | solution.py:135
  270.4 5.8 convolution_convert_fusion
  276.3 10.6 %convolution_convert_fusion.2 = bf16[768,768]{0,1:T(8,128)(2,1)} fusion(bf16[3136,768]{0,1:T(8,128)(2,1)} %all-gather.8.cloned.1.call-done, f32[3136,768]{1,0:T(8,128)} %copy-done.30, f32[768]{0:T(1024)S(1)} %dynamic_slice.12), kind=kOutput, calls=%fused_computation.54 | convolution fusion | flops 3724050432 | bytes 15633408 | tf_op jit(solution)/shard_map/dot_general | solution.py:136
  291.3 9.1 %convolution_convert_fusion.3 = bf16[768,768]{1,0:T(8,128)(2,1)} fusion(bf16[3136,768]{0,1:T(8,128)(2,1)} %all-gather.4.cloned.1.call-done, bf16[3136,768]{1,0:T(8,128)(2,1)} %copy-done.31), kind=kOutput, calls=%fused_computation.55 | convolution fusion | flops 3699965952 | bytes 10813440 | tf_op jit(solution)/shard_map/dot_general | solution.py:138
  300.4 7.7 %all-to-all-done.1 = bf16[8,768,96]{1,2,0:T(8,128)(2,1)} async-done(((bf16[8,768,96]{1,2,0:T(8,128)(2,1)}), bf16[8,768,96]{1,2,0:T(8,128)(2,1)}, u32[]{:S(2)}, u32[]{:S(2)}) %all-to-all-start.1) | async-done | bytes 1179680 | tf_op jit(solution)/shard_map/all_to_all | solution.py:40
  315.5 4.8 copy.76
  331.4 10.7 %reduce-scatter.3.cloned.1.call-done = bf16[3136,192]{0,1:T(8,128)(2,1)} async-done(((bf16[3136,768]{0,1:T(8,128)(2,1)}), bf16[3136,192]{0,1:T(8,128)(2,1)}) %reduce-scatter.3.cloned.1.call-update) | async-done | bytes 1204240 | tf_op jit(solution)/shard_map/reduce_scatter | solution.py:68
  343.7 5.7 reshape.138
  349.3 84.1 %reduce-scatter.5.cloned.1.call-done = bf16[3136,192]{0,1:T(8,128)(2,1)} async-done(((bf16[3136,768]{0,1:T(8,128)(2,1)}), bf16[3136,192]{0,1:T(8,128)(2,1)}) %reduce-scatter.5.cloned.1.call-update) | async-done | bytes 1204240 | tf_op jit(solution)/shard_map/reduce_scatter | solution.py:68
  435.8 5.7 reshape.130
  446.3 19.7 %all-reduce.3 = (f32[16,196]{1,0:T(8,128)}, f32[16,196]{1,0:T(8,128)}) all-reduce(f32[16,196]{1,0:T(8,128)S(1)} %get-tuple-element.18, f32[16,196]{1,0:T(8,128)} %reduce_sum.187), channel_id=1, replica_groups=mesh['dp'=8,'tp'=4] {'tp'}, use_global_device_ids=true, to_apply=%region_13.14 | all-reduce | flops 6272 | bytes 50176 | tf_op jit(solution)/shard_map/psum | solution.py:52
  466.7 8.6 %convert_reduce_fusion.3 = (f32[196]{0:T(256)}, f32[16,196,192]{1,2,0:T(8,128)S(1)}, bf16[16,196,192]{1,2,0:T(8,128)(2,1)}) fusion(f32[16,196,192]{1,2,0:T(8,128)} %copy.76, f32[16,196]{1,0:T(8,128)} %get-tuple-element.34, f32[16,196,192]{1,2,0:T(8,128)} %copy-done.3, f32[16,196]{1,0:T(8,128)S(1)} %get-tuple-element.47, ...), kind=kLoop, calls=%fused_computation.37 | loop fusion | flops 8429372 | bytes 13298192 | tf_op jit(solution)/shard_map/reduce_sum | solution.py:158
  475.3 6.2 convolution_bitcast_fusion
  502.5 16.1 %all-reduce.2 = (f32[16,196]{1,0:T(8,128)S(1)}, f32[16,196]{1,0:T(8,128)S(1)}) all-reduce(f32[16,196]{1,0:T(8,128)S(1)} %get-tuple-element.16, f32[16,196]{1,0:T(8,128)S(1)} %get-tuple-element.21), channel_id=1, replica_groups=mesh['dp'=8,'tp'=4] {'tp'}, use_global_device_ids=true, to_apply=%region_17.18 | all-reduce | flops 6272 | bytes 50176 | tf_op jit(solution)/shard_map/psum | solution.py:52
  518.6 5.3 add_convert_fusion
  529.2 39.9 %all-reduce = (f32[2,768]{1,0:T(2,128)S(1)}, f32[384]{0:T(512)}, f32[196]{0:T(256)}, f32[3072]{0:T(1024)}, f32[768]{0:T(1024)}) all-reduce(f32[2,768]{1,0:T(2,128)S(1)} %broadcast_multiply_fusion.6, f32[384]{0:T(512)S(1)} %copy-done.20, f32[196]{0:T(256)S(1)} %copy-done.19, ...), channel_id=1, replica_groups=mesh['dp'=8,'tp'=4] {'dp','tp'}, use_global_device_ids=true, to_apply=%region_24.25 | all-reduce | flops 5956 | bytes 47648 | tf_op jit(solution)/shard_map/psum | solution.py:172
  569.1 79.3 %all-reduce.8.cloned.1.call-done = (f32[64,2,768]{2,0,1:T(8,128)}, f32[196,384]{1,0:T(8,128)}, f32[384,196]{0,1:T(8,128)}) async-done(((f32[64,2,768]{2,0,1:T(8,128)}, f32[196,384]{1,0:T(8,128)}, f32[384,196]{0,1:T(8,128)}), (f32[64,2,768]{2,0,1:T(8,128)}, f32[196,384]{1,0:T(8,128)}, f32[384,196]{0,1:T(8,128)})) %all-reduce.8.cloned.1.call-update) | async-done | bytes 995344 | tf_op jit(solution)/shard_map/psum | solution.py:172
  (169 shorter events, 120.1 us)
Async XLA Ops:
  7.2 90.6 %all-gather.6.cloned.1.call-start = ((), (), s32[]{:S(2)}) async-start(), calls=%async_computation.5 | async-start | bytes 1327104 | tf_op jit(solution)/shard_map/all_gather | solution.py:120
  8.9 151.5 %all-gather.4.cloned.1.call-start = ((), (), s32[]{:S(2)}) async-start(), calls=%async_computation.4 | async-start | bytes 6144000 | tf_op jit(solution)/shard_map/all_gather | solution.py:64
  12.3 24.2 %copy-start.16 = (f32[192]{0:T(256)S(1)}, f32[192]{0:T(256)}, u32[]{:S(2)}) copy-start(f32[192]{0:T(256)} %param.16) | copy-start | bytes 2308
  12.3 24.2 %copy-start.21 = (f32[192]{0:T(256)S(1)}, f32[192]{0:T(256)}, u32[]{:S(2)}) copy-start(f32[192]{0:T(256)} %param.17) | copy-start | bytes 2308
  15.6 24.6 %copy-start.10 = (f32[196,384]{1,0:T(8,128)S(1)}, f32[196,384]{1,0:T(8,128)}, u32[]{:S(2)}) copy-start(f32[196,384]{1,0:T(8,128)} %param.18) | copy-start | bytes 903172
  42.1 18.4 %copy-start.14 = (f32[192]{0:T(256)S(1)}, f32[192]{0:T(256)}, u32[]{:S(2)}) copy-start(f32[192]{0:T(256)} %param.22) | copy-start | bytes 2308
  44.6 19.2 %copy-start.3 = (f32[16,196,192]{1,2,0:T(8,128)}, f32[16,196,192]{1,2,0:T(8,128)S(1)}, u32[]{:S(2)}) copy-start(f32[16,196,192]{1,2,0:T(8,128)S(1)} %get-tuple-element.55) | copy-start | bytes 7225348
  68.1 184.9 %all-gather.8.cloned.1.call-start = ((), (), s32[]{:S(2)}) async-start(), calls=%async_computation.7 | async-start | bytes 6144000 | tf_op jit(solution)/shard_map/all_gather | solution.py:64
  73.3 268.9 %reduce-scatter.3.cloned.1.call-start = ((), (), s32[]{:S(2)}) async-start(), calls=%async_computation.6 | async-start | bytes 6144000 | tf_op jit(solution)/shard_map/reduce_scatter | solution.py:68
  74.1 5.7 collective-permute-start
  74.1 5.9 collective-permute-start.1
  79.8 6.1 collective-permute-start.2
  80.0 5.9 collective-permute-start.3
  85.8 6.4 collective-permute-start.4
  85.8 6.4 collective-permute-start.5
  92.3 5.5 collective-permute-start.6
  177.8 255.6 %reduce-scatter.5.cloned.1.call-start = ((), (), s32[]{:S(2)}) async-start(), calls=%async_computation.8 | async-start | bytes 6144000 | tf_op jit(solution)/shard_map/reduce_scatter | solution.py:68
  253.1 17.4 %copy-start.24 = (bf16[768,768]{1,0:T(8,128)(2,1)S(1)}, bf16[768,768]{1,0:T(8,128)(2,1)}, u32[]{:S(2)}) copy-start(bf16[768,768]{1,0:T(8,128)(2,1)} %all-gather.6.cloned.1.call-done) | copy-start | bytes 3538948
  286.9 21.3 %all-to-all-start.1 = ((bf16[8,768,96]{1,2,0:T(8,128)(2,1)}), bf16[8,768,96]{1,2,0:T(8,128)(2,1)}, u32[]{:S(2)}, u32[]{:S(2)}) async-start(bf16[8,768,96]{1,2,0:T(8,128)(2,1)} %bitcast.19), calls=%async_computation.3 | async-start | bytes 2359296 | tf_op jit(solution)/shard_map/all_to_all | solution.py:40
  308.2 21.1 %all-to-all-start = ((bf16[8,96,768]{2,1,0:T(8,128)(2,1)}), bf16[8,96,768]{2,1,0:T(8,128)(2,1)}, u32[]{:S(2)}, u32[]{:S(2)}) async-start(bf16[8,96,768]{2,1,0:T(8,128)(2,1)} %bitcast.94), calls=%async_computation.2 | async-start | bytes 2359296 | tf_op jit(solution)/shard_map/all_to_all | solution.py:40
  312.4 336.0 %all-reduce.8.cloned.1.call-start = ((), (), s32[]{:S(2)}) async-start(), calls=%async_computation.9 | async-start | bytes 2015232 | tf_op jit(solution)/shard_map/psum | solution.py:172
  343.6 89.8 %copy-start.15 = (f32[192]{0:T(256)S(1)}, f32[192]{0:T(256)}, u32[]{:S(2)}) copy-start(f32[192]{0:T(256)} %param.22) | copy-start | bytes 2308
  496.6 22.0 %copy-start.2 = (f32[16,196,192]{1,2,0:T(8,128)S(1)}, f32[16,196,192]{1,2,0:T(8,128)}, u32[]{:S(2)}) copy-start(f32[16,196,192]{1,2,0:T(8,128)} %copy.70) | copy-start | bytes 7225348
  496.6 22.0 %copy-start.18 = (f32[192]{0:T(256)S(1)}, f32[192]{0:T(256)}, u32[]{:S(2)}) copy-start(f32[192]{0:T(256)} %param.16) | copy-start | bytes 2308
  (25 other events, 112.2 us)
Sparse Core Ops, SparseCore 0:
  10.5 26.7 all-gather.5
  68.2 92.0 all-gather.3
  161.9 91.0 all-gather.7
  255.2 86.8 reduce-scatter.2
  344.4 88.9 reduce-scatter.4
  518.7 129.7 all-reduce.7
